TPU v7x, 32 devices: a whole 2x2x4 slice. The times are simulated.
32 devices in a mesh: ep: 8 (over z, x), tp: 4 (over y, core).
Axes of the slice: x: 2, y: 2, z: 4, core: 2. Of those that a mesh axis runs over, the one named last changes fastest.
Arguments:
- hidden_in: bfloat16 [1024, 2048], P('ep', 'tp'), may hold values from -6 to 6
- norm_gain: float32 [2048], replicated, may hold values from 0.5 to 1.5
- router_weight: bfloat16 [2048, 8], replicated, may hold values from -4.861359 to 4.861359
- shared_gate_up: bfloat16 [2048, 2, 1408], P(None, None, 'tp'), may hold values from -0.125 to 0.125
- shared_down: bfloat16 [1408, 2048], P('tp'), may hold values from -0.15625 to 0.15625
- slot_gate_up: bfloat16 [32, 2048, 2, 704], P(('ep', 'tp')), as said below
- slot_down: bfloat16 [32, 704, 2048], P(('ep', 'tp')), as said below
- slot_expert: int32 [32], replicated, may hold values from 0 to 7, as said below
- slot_choice: int32 [1024, 6], P('ep'), may hold values from 0 to 31, all different within a row; in each aligned block of 32 rows (0 to 31, 32 to 63, ...) at most 12 rows name the same one
- live_count: int32 [8], P('ep'), may hold values from 64 to 128, as said below
Outputs:
- mixed_out: bfloat16 [1024, 2048], P('ep', 'tp')
Inputs may be any that keep to these rules, and one draw needn't show every extreme that they name: `slot_expert`: each expert is held by 1 or 7 slots; exactly 4 experts by the larger number. `slot_gate_up`: entry s holds the weights of expert slot_expert[s]; slots of one expert hold equal weights. `slot_down`: entry s holds the weights of expert slot_expert[s]; slots of one expert hold equal weights. `slot_choice`: a row names 6 different slots; in each aligned block of 32 rows no slot is named more than 12 times. `live_count`: the live rows of an index of ep are its first ones; some index of ep has all 128 rows live.
All inputs are finite; a program needn't handle non-finite values.
Results may differ from a plain program's by a relative error of at most 0.0058.
Values may be sent and summed in bfloat16 or wider, within the bound.
A program may use at most 64 MiB of HBM per device.

v0:
```python
import jax
import jax.numpy as jnp
from jax import lax
from jax.sharding import PartitionSpec as P


def gate_weights(normed_rows, choices, router_weight, slot_expert):
    logits = jnp.dot(normed_rows, router_weight, preferred_element_type=jnp.float32)
    slot_total = slot_expert.shape[0]
    expert_total = router_weight.shape[1]
    slot_hit = choices[:, :, None] == jnp.arange(slot_total, dtype=jnp.int32)
    expert_ids = jnp.sum(jnp.where(slot_hit, slot_expert, 0), axis=2)
    expert_hit = expert_ids[:, :, None] == jnp.arange(expert_total, dtype=jnp.int32)
    picked = jnp.sum(jnp.where(expert_hit, logits[:, None, :], 0.0), axis=2)
    highest = jnp.max(picked, axis=1, keepdims=True)
    weights = jnp.exp(picked - highest)
    return (weights / jnp.sum(weights, axis=1, keepdims=True)).astype(jnp.bfloat16)


def slot_positions(targets):
    length = targets.shape[0]
    same_slot = targets[:, None] == targets[None, :]
    earlier = jnp.arange(length)[None, :] < jnp.arange(length)[:, None]
    return jnp.sum(same_slot & earlier, axis=1)


def expert_apply(received, slot_gate_up, slot_down):
    shape_in = received.shape
    flat_rows = received.reshape(-1, shape_in[-1])
    gate_up = jnp.einsum(
        "rd,dgf->rgf", flat_rows, slot_gate_up[0], preferred_element_type=jnp.float32
    )
    activated = (jax.nn.silu(gate_up[:, 0]) * gate_up[:, 1]).astype(jnp.bfloat16)
    result = jnp.dot(activated, slot_down[0], preferred_element_type=jnp.float32).astype(
        jnp.bfloat16
    )
    return result.reshape(shape_in)


def local(
    hidden_in,
    norm_gain,
    router_weight,
    shared_gate_up,
    shared_down,
    slot_gate_up,
    slot_down,
    slot_expert,
    slot_choice,
    live_count,
):
    tp_count = lax.axis_size("tp")
    ep_count = lax.axis_size("ep")
    tp_index = lax.axis_index("tp")
    tok_count = hidden_in.shape[0]
    feature_width = hidden_in.shape[1] * tp_count
    top_count = slot_choice.shape[1]
    slot_count = slot_expert.shape[0]
    quarter = tok_count // tp_count
    capacity = max(2, 2 * quarter * top_count // slot_count)
    full_rows = lax.all_gather(hidden_in, "tp", axis=1, tiled=True)
    wide_rows = full_rows.astype(jnp.float32)
    norm_scale = lax.rsqrt(jnp.mean(wide_rows * wide_rows, axis=1, keepdims=True) + 1e-06)
    normed = (wide_rows * norm_scale * norm_gain).astype(jnp.bfloat16)
    shared_proj = jnp.einsum(
        "td,dgf->tgf", normed, shared_gate_up, preferred_element_type=jnp.float32
    )
    shared_hidden = (jax.nn.silu(shared_proj[:, 0]) * shared_proj[:, 1]).astype(jnp.bfloat16)
    partial_value = jnp.dot(shared_hidden, shared_down, preferred_element_type=jnp.float32)
    row_start = tp_index * quarter
    own_rows = lax.dynamic_slice_in_dim(normed, row_start, quarter, 0)
    own_choice = lax.dynamic_slice_in_dim(slot_choice, row_start, quarter, 0)
    gate_values = gate_weights(own_rows, own_choice, router_weight, slot_expert)
    targets = own_choice.reshape(-1)
    placed = targets * capacity + slot_positions(targets)
    outgoing = jnp.zeros((slot_count * capacity, feature_width), jnp.bfloat16)
    outgoing = outgoing.at[placed].set(jnp.repeat(own_rows, top_count, axis=0))
    outgoing = outgoing.reshape(ep_count, tp_count, capacity, feature_width)
    arrived = lax.all_to_all(
        lax.all_to_all(outgoing, "ep", split_axis=0, concat_axis=0, tiled=True),
        "tp",
        split_axis=1,
        concat_axis=1,
        tiled=True,
    )
    computed = expert_apply(arrived, slot_gate_up, slot_down)
    returned = lax.all_to_all(
        lax.all_to_all(computed, "ep", split_axis=0, concat_axis=0, tiled=True),
        "tp",
        split_axis=1,
        concat_axis=1,
        tiled=True,
    )
    fetched = returned.reshape(-1, feature_width)[placed].reshape(quarter, top_count, feature_width)
    routed = jnp.einsum("qk,qkd->qd", gate_values, fetched, preferred_element_type=jnp.float32)
    own_partial = lax.dynamic_slice_in_dim(partial_value, row_start, quarter, 0) + routed
    partial_value = lax.dynamic_update_slice_in_dim(partial_value, own_partial, row_start, 0)
    summed = lax.psum_scatter(partial_value, "tp", scatter_dimension=1, tiled=True)
    live_rows = jnp.arange(tok_count, dtype=jnp.int32) < live_count[0]
    mixed_out = jnp.where(live_rows[:, None], hidden_in.astype(jnp.float32) + summed, 0.0)
    return mixed_out.astype(jnp.bfloat16)


def solution(mesh):
    in_specs = (
        P("ep", "tp"),
        P(),
        P(),
        P(None, None, "tp"),
        P("tp", None),
        P(("ep", "tp"), None, None, None),
        P(("ep", "tp"), None, None),
        P(),
        P("ep", None),
        P("ep"),
    )
    out_specs = P("ep", "tp")
    return jax.shard_map(local, mesh=mesh, in_specs=in_specs, out_specs=out_specs, check_vma=False)
```

profile of v0, /device:TPU:0, one launch (start us, length us, event | category | flops | bytes accessed | tf_op | source)
XLA Modules:
  0.0 238.2 jit_solution(8258291260687447549)
XLA Ops:
  6.5 9.0 %all_gather.3 = bf16[128,2048]{1,0:T(8,128)(2,1)S(1)} all-gather(bf16[128,512]{1,0:T(8,128)(2,1)} %param.10), channel_id=1, replica_groups=mesh['ep'=8,'tp'=4] {'tp'}, dimensions={1}, use_global_device_ids=true | all-gather | bytes 655360 | tf_op jit(solution)/shard_map/all_gather | solution.py:61
  15.7 0.9 fusion.10
  16.6 0.8 copy-done.1
  18.1 1.1 broadcast_in_dim.58
  19.2 2.2 reshape.86
  21.4 3.7 %scatter_custom_fusion = bf16[384,2048]{1,0:T(8,128)(2,1)} fusion(s32[192]{0:T(256)S(1)} %bitcast.43, bf16[192,2048]{1,0:T(8,128)(2,1)} %reshape.86, bf16[]{:T(256)} %constant.10.clone.1), kind=kCustom, calls=%fused_computation.14 | custom fusion | bytes 1573376 | tf_op jit(solution)/shard_map/scatter | solution.py:77
  25.1 3.6 %reshape.69 = bf16[8,4,12,2048]{3,2,1,0:T(8,128)(2,1)} reshape(bf16[384,2048]{1,0:T(8,128)(2,1)} %scatter_custom_fusion) | data formatting | bytes 3145728 | tf_op jit(solution)/shard_map/reshape | solution.py:78
  28.7 2.8 %copy.29 = bf16[8,4,12,2048]{3,1,2,0:T(4,128)(2,1)S(1)} copy(bf16[8,4,12,2048]{3,2,1,0:T(8,128)(2,1)} %reshape.69) | data formatting | bytes 3145728 | tf_op jit(solution)/shard_map/reshape | solution.py:78
  31.5 43.1 %all_to_all.20 = bf16[8,4,12,2048]{3,1,2,0:T(4,128)(2,1)S(1)} all-to-all(bf16[8,4,12,2048]{3,1,2,0:T(4,128)(2,1)S(1)} %copy.29), channel_id=1, replica_groups=mesh['ep'=8,'tp'=4] {'ep'}, dimensions={0} | all-to-all | bytes 3145728 | tf_op jit(solution)/shard_map/all_to_all | solution.py:80
  74.6 0.9 copy.30
  75.5 22.5 %all_to_all.21 = bf16[8,4,12,2048]{3,0,2,1:T(8,128)(2,1)S(1)} all-to-all(bf16[8,4,12,2048]{3,0,2,1:T(8,128)(2,1)S(1)} %copy.30), channel_id=1, replica_groups=mesh['ep'=8,'tp'=4] {'tp'}, dimensions={1} | all-to-all | bytes 3145728 | tf_op jit(solution)/shard_map/all_to_all | solution.py:79
  98.0 2.2 copy.31
  100.3 3.6 %reshape.91 = bf16[384,2048,1]{1,0,2:T(8,128)(2,1)} reshape(bf16[8,4,12,2048]{3,2,1,0:T(8,128)(2,1)} %copy.31) | data formatting | bytes 3145728 | tf_op jit(solution)/shard_map/reshape | solution.py:29
  103.9 5.6 %fusion = f32[384,2,704]{0,2,1:T(8,128)S(1)} fusion(bf16[384,2048,1]{1,0,2:T(8,128)(2,1)} %reshape.91, bf16[1,2048,2,704]{1,3,2,0:T(8,128)(2,1)} %param.15), kind=kOutput, calls=%fused_computation.2 | convolution fusion | flops 2214592512 | bytes 9502720 | tf_op jit(solution)/shard_map/rd,dgf->rgf/dot_general | solution.py:30
  109.5 2.6 %fusion.4 = bf16[384,2048]{1,0:T(8,128)(2,1)} fusion(bf16[1,704,2048]{2,1,0:T(8,128)(2,1)S(1)} %copy-done, f32[384,2,704]{0,2,1:T(8,128)S(1)} %fusion), kind=kOutput, calls=%fused_computation.6 | convolution fusion | flops 1109704704 | bytes 6619136 | tf_op jit(solution)/shard_map/dot_general | solution.py:34
  112.2 3.6 %reshape.71 = bf16[8,4,12,2048]{3,2,1,0:T(8,128)(2,1)} reshape(bf16[384,2048]{1,0:T(8,128)(2,1)} %fusion.4) | data formatting | bytes 3145728 | tf_op jit(solution)/shard_map/reshape | solution.py:37
  115.8 4.0 %copy.32 = bf16[8,4,12,2048]{3,1,2,0:T(4,128)(2,1)} copy(bf16[8,4,12,2048]{3,2,1,0:T(8,128)(2,1)} %reshape.71) | data formatting | bytes 3145728 | tf_op jit(solution)/shard_map/reshape | solution.py:37
  119.7 4.6 %all-to-all-start.2 = ((bf16[8,4,12,2048]{3,1,2,0:T(4,128)(2,1)}), bf16[8,4,12,2048]{3,1,2,0:T(4,128)(2,1)}, u32[]{:S(2)}, u32[]{:S(2)}) async-start(bf16[8,4,12,2048]{3,1,2,0:T(4,128)(2,1)} %copy.32), calls=%async_computation.2 | async-start | bytes 3145728 | tf_op jit(solution)/shard_map/all_to_all | solution.py:88
  124.5 36.6 %all-to-all-done.2 = bf16[8,4,12,2048]{3,1,2,0:T(4,128)(2,1)} async-done(((bf16[8,4,12,2048]{3,1,2,0:T(4,128)(2,1)}), bf16[8,4,12,2048]{3,1,2,0:T(4,128)(2,1)}, u32[]{:S(2)}, u32[]{:S(2)}) %all-to-all-start.2) | async-done | bytes 1572896 | tf_op jit(solution)/shard_map/all_to_all | solution.py:88
  161.1 3.4 %copy.33 = bf16[8,4,12,2048]{3,0,2,1:T(8,128)(2,1)} copy(bf16[8,4,12,2048]{3,1,2,0:T(4,128)(2,1)} %all-to-all-done.2) | data formatting | bytes 3145728 | tf_op jit(solution)/shard_map/all_to_all | solution.py:88
  164.5 4.5 %all-to-all-start.3 = ((bf16[8,4,12,2048]{3,0,2,1:T(8,128)(2,1)}), bf16[8,4,12,2048]{3,0,2,1:T(8,128)(2,1)}, u32[]{:S(2)}, u32[]{:S(2)}) async-start(bf16[8,4,12,2048]{3,0,2,1:T(8,128)(2,1)} %copy.33), calls=%async_computation.3 | async-start | bytes 3145728 | tf_op jit(solution)/shard_map/all_to_all | solution.py:87
  169.5 2.8 %fusion.15 = f32[128,2,352]{0,2,1:T(8,128)S(1)} fusion(bf16[2048,2,352]{0,2,1:T(8,128)(2,1)} %param.13, bf16[128,2048]{1,0:T(8,128)(2,1)S(1)} %copy-done.2), kind=kOutput, calls=%fused_computation.17 | convolution fusion | flops 369098752 | bytes 3768320 | tf_op jit(solution)/shard_map/td,dgf->tgf/dot_general | solution.py:65
  172.4 1.5 fusion.21
  173.9 15.2 %all-to-all-done.3 = bf16[8,4,12,2048]{3,0,2,1:T(8,128)(2,1)} async-done(((bf16[8,4,12,2048]{3,0,2,1:T(8,128)(2,1)}), bf16[8,4,12,2048]{3,0,2,1:T(8,128)(2,1)}, u32[]{:S(2)}, u32[]{:S(2)}) %all-to-all-start.3) | async-done | bytes 1572896 | tf_op jit(solution)/shard_map/all_to_all | solution.py:87
  189.1 3.6 %copy.34 = bf16[8,4,12,2048]{3,2,1,0:T(8,128)(2,1)} copy(bf16[8,4,12,2048]{3,0,2,1:T(8,128)(2,1)} %all-to-all-done.3) | data formatting | bytes 3145728 | tf_op jit(solution)/shard_map/all_to_all | solution.py:87
  192.8 3.6 %reshape.72 = bf16[384,2048]{1,0:T(8,128)(2,1)} reshape(bf16[8,4,12,2048]{3,2,1,0:T(8,128)(2,1)} %copy.34) | data formatting | bytes 3145728 | tf_op jit(solution)/shard_map/reshape | solution.py:94
  196.4 4.4 %gather_fusion = bf16[192,2048]{1,0:T(8,128)(2,1)} fusion(bf16[384,2048]{1,0:T(8,128)(2,1)} %reshape.72, s32[1024]{0:T(1024)S(1)} %pad_clamp_fusion), kind=kCustom, calls=%fused_computation | custom fusion | bytes 1573632 | tf_op jit(solution)/shard_map/gather | solution.py:94
  200.8 2.2 reshape.73
  203.0 1.7 fusion.29
  204.7 1.7 fusion.17
  207.1 22.5 %reduce-scatter.2.cloned.1.call-done = f32[128,512]{1,0:T(8,128)} async-done(((f32[128,2048]{1,0:T(8,128)}), f32[128,512]{1,0:T(8,128)}) %reduce-scatter.2.cloned.1.call-update) | async-done | bytes 262160 | tf_op jit(solution)/shard_map/reduce_scatter | solution.py:98
  229.6 1.7 select_convert_fusion
  (36 shorter events, 1.5 us)
Async XLA Ops:
  6.5 103.0 %copy-start = (bf16[1,704,2048]{2,1,0:T(8,128)(2,1)S(1)}, bf16[1,704,2048]{2,1,0:T(8,128)(2,1)}, u32[]{:S(2)}) copy-start(bf16[1,704,2048]{2,1,0:T(8,128)(2,1)} %param.16) | copy-start | bytes 8650756
  6.5 10.9 %copy-start.6 = (s32[128,6]{0,1:T(8,128)S(1)}, s32[128,6]{0,1:T(8,128)}, u32[]{:S(2)}) copy-start(s32[128,6]{0,1:T(8,128)} %param.18) | copy-start | bytes 9220
  16.6 0.8 copy-start.1
  119.7 4.6 %copy-start.5 = (bf16[2048,8]{0,1:T(8,128)(2,1)S(1)}, bf16[2048,8]{0,1:T(8,128)(2,1)}, u32[]{:S(2)}) copy-start(bf16[2048,8]{0,1:T(8,128)(2,1)} %param.12) | copy-start | bytes 98308
  119.7 41.3 %all-to-all-start.2 = ((bf16[8,4,12,2048]{3,1,2,0:T(4,128)(2,1)}), bf16[8,4,12,2048]{3,1,2,0:T(4,128)(2,1)}, u32[]{:S(2)}, u32[]{:S(2)}) async-start(bf16[8,4,12,2048]{3,1,2,0:T(4,128)(2,1)} %copy.32), calls=%async_computation.2 | async-start | bytes 3145728 | tf_op jit(solution)/shard_map/all_to_all | solution.py:88
  164.5 4.5 %copy-start.7 = (s32[32]{0:T(128)S(1)}, s32[32]{0:T(128)}, u32[]{:S(2)}) copy-start(s32[32]{0:T(128)} %param.17) | copy-start | bytes 388
  164.5 5.0 %copy-start.2 = (bf16[128,2048]{1,0:T(8,128)(2,1)S(1)}, bf16[128,2048]{1,0:T(8,128)(2,1)}, u32[]{:S(2)}) copy-start(bf16[128,2048]{1,0:T(8,128)(2,1)} %copy-done.1) | copy-start | bytes 1572868
  164.5 24.6 %all-to-all-start.3 = ((bf16[8,4,12,2048]{3,0,2,1:T(8,128)(2,1)}), bf16[8,4,12,2048]{3,0,2,1:T(8,128)(2,1)}, u32[]{:S(2)}, u32[]{:S(2)}) async-start(bf16[8,4,12,2048]{3,0,2,1:T(8,128)(2,1)} %copy.33), calls=%async_computation.3 | async-start | bytes 3145728 | tf_op jit(solution)/shard_map/all_to_all | solution.py:87
  169.0 60.6 %reduce-scatter.2.cloned.1.call-start = ((), (), s32[]{:S(2)}) async-start(), calls=%async_computation.5 | async-start | bytes 1310720 | tf_op jit(solution)/shard_map/reduce_scatter | solution.py:98
  169.5 2.9 %copy-start.3 = (bf16[352,2048]{1,0:T(8,128)(2,1)S(1)}, bf16[352,2048]{1,0:T(8,128)(2,1)}, u32[]{:S(2)}) copy-start(bf16[352,2048]{1,0:T(8,128)(2,1)} %param.14) | copy-start | bytes 4325380
  203.0 26.6 %copy-start.4 = (bf16[128,512]{1,0:T(8,128)(2,1)S(1)}, bf16[128,512]{1,0:T(8,128)(2,1)}, u32[]{:S(2)}) copy-start(bf16[128,512]{1,0:T(8,128)(2,1)} %param.10) | copy-start | bytes 393220
Sparse Core Ops, SparseCore 0:
  206.6 22.9 reduce-scatter.1
where the time goes:
time: 239 us; the launch traced here: 238 us
  blocking collectives  74.6 us (31%)
  waiting for transfers between devices  74.3 us (31%)
  local copies, waits for them, and re-layouts  46.3 us (19%)
  matrix products  14.5 us (6%)
  between operations  14.2 us (6%)
  starting transfers between devices  9.12 us (4%)
  other arithmetic  5.13 us (2%)
    all_to_all x1, blocking collectives, local(): lax.all_to_all(outgoing, 'ep', split_axis=0, concat_axis=0, tiled=True)  43.1 us
    all_to_all x1, waiting for transfers between devices, local(): lax.all_to_all(computed, 'ep', split_axis=0, concat_axis=0, tiled=True)  36.6 us
    all_to_all x1, blocking collectives, local(): lax.all_to_all(lax.all_to_all(outgoing, 'ep', split_axis=0, concat_axis=0...  22.5 us
    reduce_scatter x1, waiting for transfers between devices, local(): lax.psum_scatter(partial_value, 'tp', scatter_dimension=1, tiled=True)  22.5 us
    all_to_all x1, waiting for transfers between devices, local(): lax.all_to_all(lax.all_to_all(computed, 'ep', split_axis=0, concat_axis=0...  15.2 us
    all_gather x1, blocking collectives, local(): full_rows = lax.all_gather(hidden_in, 'tp', axis=1, tiled=True)  8.98 us
    reshape x2, local copies, waits for them, and re-layouts, expert_apply(): return result.reshape(shape_in)  7.55 us
    reshape x2, local copies, waits for them, and re-layouts, local(): outgoing = outgoing.reshape(ep_count, tp_count, capacity, feature_width)  6.42 us
  transfers between devices with their start and end apart: 3, of which 3 were waited for; matrix products, arithmetic and copies ran while one was open for 2% of the time, Pallas kernels for 0%

commit v1 on v0

--- a/solution.py
+++ b/solution.py
@@ -37,7 +37,7 @@
     return result.reshape(shape_in)
 
 
-def local(
+def local_exchange(
     hidden_in,
     norm_gain,
     router_weight,
@@ -101,6 +101,73 @@
     return mixed_out.astype(jnp.bfloat16)
 
 
+def local_dense(
+    hidden_in,
+    norm_gain,
+    router_weight,
+    shared_gate_up,
+    shared_down,
+    slot_gate_up,
+    slot_down,
+    slot_expert,
+    slot_choice,
+    live_count,
+):
+    tp_count = lax.axis_size("tp")
+    ep_count = lax.axis_size("ep")
+    ep_index = lax.axis_index("ep")
+    me = ep_index * tp_count + lax.axis_index("tp")
+    tok_count, part_width = hidden_in.shape
+    feature_width = part_width * tp_count
+    top_count = slot_choice.shape[1]
+    slot_count = slot_expert.shape[0]
+    quarter = tok_count // tp_count
+    capacity = tp_count * max(2, 2 * quarter * top_count // slot_count)
+    blocks = lax.all_gather(hidden_in, ("ep", "tp"), axis=0)
+    choices = lax.all_gather(slot_choice, "ep", axis=0, tiled=True)
+    blocks = blocks.reshape(ep_count, tp_count, tok_count, part_width)
+    full_rows = blocks.transpose(0, 2, 1, 3).reshape(ep_count * tok_count, feature_width)
+    wide_rows = full_rows.astype(jnp.float32)
+    norm_scale = lax.rsqrt(jnp.mean(wide_rows * wide_rows, axis=1, keepdims=True) + 1e-06)
+    normed = (wide_rows * norm_scale * norm_gain).astype(jnp.bfloat16)
+    gate_values = gate_weights(normed, choices, router_weight, slot_expert)
+    mine = choices == me
+    hit = jnp.any(mine, axis=1).reshape(ep_count, tok_count)
+    gate = jnp.sum(jnp.where(mine, gate_values, 0).astype(jnp.float32), axis=1)
+    gate = gate.reshape(ep_count, tok_count)
+    earlier = jnp.arange(tok_count)[:, None] < jnp.arange(tok_count)[None, :]
+    place = jnp.dot(
+        hit.astype(jnp.bfloat16), earlier.astype(jnp.bfloat16), preferred_element_type=jnp.float32
+    ).astype(jnp.int32)
+    chosen = hit[:, None, :] & (place[:, None, :] == jnp.arange(capacity)[None, :, None])
+    blocked = normed.reshape(ep_count, tok_count, feature_width)
+    picked = jnp.einsum(
+        "bcr,brd->bcd",
+        chosen.astype(jnp.bfloat16),
+        blocked,
+        preferred_element_type=jnp.float32,
+    ).astype(jnp.bfloat16)
+    computed = expert_apply(picked, slot_gate_up, slot_down)
+    spread = jnp.where(chosen, gate[:, None, :], 0.0).astype(jnp.bfloat16)
+    routed = jnp.einsum("bcr,bcd->brd", spread, computed, preferred_element_type=jnp.float32)
+    own_rows = lax.dynamic_index_in_dim(blocked, ep_index, 0, keepdims=False)
+    shared_proj = jnp.einsum(
+        "td,dgf->tgf", own_rows, shared_gate_up, preferred_element_type=jnp.float32
+    )
+    shared_hidden = (jax.nn.silu(shared_proj[:, 0]) * shared_proj[:, 1]).astype(jnp.bfloat16)
+    shared_part = jnp.dot(shared_hidden, shared_down, preferred_element_type=jnp.float32)
+    own_block = jnp.arange(ep_count)[:, None, None] == ep_index
+    partial = (routed + jnp.where(own_block, shared_part[None], 0.0)).astype(jnp.bfloat16)
+    partial = partial.reshape(ep_count, tok_count, tp_count, part_width).transpose(0, 2, 1, 3)
+    partial = partial.reshape(ep_count * tp_count, tok_count, part_width)
+    summed = lax.psum_scatter(partial, ("ep", "tp"), scatter_dimension=0)
+    live_rows = jnp.arange(tok_count, dtype=jnp.int32) < live_count[0]
+    mixed_out = jnp.where(
+        live_rows[:, None], hidden_in.astype(jnp.float32) + summed.astype(jnp.float32), 0.0
+    )
+    return mixed_out.astype(jnp.bfloat16)
+
+
 def solution(mesh):
     in_specs = (
         P("ep", "tp"),
@@ -115,4 +182,5 @@
         P("ep"),
     )
     out_specs = P("ep", "tp")
+    local = local_dense if mesh.size <= 64 else local_exchange
     return jax.shard_map(local, mesh=mesh, in_specs=in_specs, out_specs=out_specs, check_vma=False)

time: 239 us -> 267 us (1.12)
  waiting for transfers between devices: 74.3 us -> 174 us
  blocking collectives: 74.6 us -> 32.5 us
  local copies, waits for them, and re-layouts: 46.3 us -> 18.1 us
  starting transfers between devices: 9.12 us -> 0.04 us
  other arithmetic: 5.13 us -> 12 us
    reduce_scatter x1, waiting for transfers between devices: 22.5 us -> 139 us  [local_dense(): summed = lax.psum_scatter(partial, ('ep', 'tp'), scatter_dimension=0)]
    all_to_all x2 -> x0, blocking collectives: 65.6 us -> none  [the longest x1 43.1 us: local(): lax.all_to_all(outgoing, 'ep', split_axis=0, concat_axis=0, tiled=True)]
    all_to_all x2 -> x0, waiting for transfers between devices: 51.8 us -> none  [the longest x1 36.6 us: local(): lax.all_to_all(computed, 'ep', split_axis=0, concat_axis=0, tiled=True)]
    all_gather x0 -> x1, waiting for transfers between devices: none -> 34.4 us  [local_dense(): blocks = lax.all_gather(hidden_in, ('ep', 'tp'), axis=0)]
    reshape x8 -> x0, local copies, waits for them, and re-layouts: 25.6 us -> none  [the longest x2 7.55 us: expert_apply(): return result.reshape(shape_in)]
    all_gather x1, blocking collectives: 8.98 us -> 32.5 us  [local_dense(): choices = lax.all_gather(slot_choice, 'ep', axis=0, tiled=True)]
    convert_element_type x1 -> x2, local copies, waits for them, and re-layouts: 0.11 us -> 17.3 us  [local_dense(): wide_rows = full_rows.astype(jnp.float32)]
    all_to_all x4 -> x0, local copies, waits for them, and re-layouts: 10.1 us -> none  [the longest x1 3.62 us: local(): lax.all_to_all(lax.all_to_all(computed, 'ep', split_axis=0, concat_axis=0...]
  transfers between devices with their start and end apart: 3 -> 2, of which waited for: 3 -> 2; matrix products, arithmetic and copies ran while one was open for 2% -> 0% of each run, Pallas kernels for 0% -> 0%
where the time goes in v1:
time: 267 us
  waiting for transfers between devices  174 us (65%)
  blocking collectives  32.5 us (12%)
  local copies, waits for them, and re-layouts  18.1 us (7%)
  matrix products  16 us (6%)
  between operations  14.2 us (5%)
  other arithmetic  12 us (4%)
    reduce_scatter x1, waiting for transfers between devices, local_dense(): summed = lax.psum_scatter(partial, ('ep', 'tp'), scatter_dimension=0)  139 us
    all_gather x1, waiting for transfers between devices, local_dense(): blocks = lax.all_gather(hidden_in, ('ep', 'tp'), axis=0)  34.4 us
    all_gather x1, blocking collectives, local_dense(): choices = lax.all_gather(slot_choice, 'ep', axis=0, tiled=True)  32.5 us
    convert_element_type x2, local copies, waits for them, and re-layouts, local_dense(): wide_rows = full_rows.astype(jnp.float32)  17.3 us
    dot_general x1, matrix products, gate_weights(): jnp.dot(normed_rows, router_weight, preferred_element_type=jnp.float32)  5.69 us
  transfers between devices with their start and end apart: 2, of which 2 were waited for; matrix products, arithmetic and copies ran while one was open for 0% of the time, Pallas kernels for 0%

profile of v1, /device:TPU:0, one launch (start us, length us, event | category | flops | bytes accessed | tf_op | source)
XLA Modules:
  0.0 266.7 jit_solution(10354327517453880037)
XLA Ops:
  6.5 0.0 copy-start
  6.5 0.0 all-gather.3.cloned.1.call-start
  6.5 0.7 all-gather.3.cloned.1.call-update
  7.3 0.0 reduce-scatter.2.cloned.1.call-start
  7.3 32.5 %all_gather.9 = s32[1024,6]{0,1:T(8,128)S(1)} all-gather(s32[128,6]{0,1:T(8,128)} %param.18), channel_id=1, replica_groups=mesh['ep'=8,'tp'=4] {'ep'}, dimensions={0}, use_global_device_ids=true | all-gather | bytes 27648 | tf_op jit(solution)/shard_map/all_gather | solution.py:127
  39.9 0.9 select_reduce_fusion
  40.7 34.4 %all-gather.3.cloned.1.call-done = bf16[4096,512]{1,0:T(8,128)(2,1)} async-done(((bf16[128,512]{1,0:T(8,128)(2,1)}), bf16[4096,512]{1,0:T(8,128)(2,1)}) %all-gather.3.cloned.1.call-update) | async-done | bytes 4194320 | tf_op jit(solution)/shard_map/all_gather | solution.py:126
  75.1 8.0 %copy.20 = f32[8,4,128,512]{2,0,3,1:T(8,128)} copy(bf16[8,4,128,512]{3,2,1,0:T(8,128)(2,1)} %bitcast.68) | data formatting | bytes 12582912 | tf_op jit(solution)/shard_map/convert_element_type | solution.py:130
  83.1 3.1 %multiply_reduce_fusion = f32[4096]{0:T(1024)S(1)} fusion(bf16[4096,512]{1,0:T(8,128)(2,1)} %all-gather.3.cloned.1.call-done), kind=kLoop, calls=%fused_computation.3 | loop fusion | flops 6287360 | bytes 4210688 | tf_op jit(solution)/shard_map/reduce_sum | solution.py:131
  86.2 0.0 copy-done.4
  86.2 0.0 copy-done.5
  86.2 5.7 %fusion.4 = f32[1024,8]{0,1:T(8,128)S(1)} fusion(bf16[2048,8]{0,1:T(8,128)(2,1)S(1)} %copy-done.4, f32[256,8,8,128]{3,2,1,0:T(8,128)} %bitcast.66, f32[2048]{0:T(1024)S(1)} %copy-done.5, f32[1024]{0:T(1024)S(1)} %get-tuple-element.11), kind=kOutput, calls=%fused_computation.9 | convolution fusion | flops 39845888 | bytes 8466432 | tf_op jit(solution)/shard_map/dot_general | solution.py:8
  91.9 0.1 select_reduce_fusion.1
  92.1 0.1 convolution_convert_fusion.1
  92.3 9.3 %copy.22 = f32[8,128,2048]{2,1,0:T(8,128)} copy(f32[8,128,2048]{1,0,2:T(8,128)} %bitcast.67) | data formatting | bytes 16777216 | tf_op jit(solution)/shard_map/convert_element_type | solution.py:130
  101.5 4.1 %multiply_convert_fusion = bf16[8,128,2048]{2,1,0:T(8,128)(2,1)S(1)} fusion(f32[8,128,2048]{2,1,0:T(8,128)} %copy.22, f32[2048]{0:T(1024)S(1)} %copy-done.5, f32[8,128]{1,0:T(8,128)S(1)} %get-tuple-element.12), kind=kLoop, calls=%fused_computation.5 | loop fusion | flops 6291456 | bytes 12595200 | tf_op jit(solution)/shard_map/convert_element_type | solution.py:132
  105.7 0.7 convolution_convert_fusion
  106.4 5.2 %fusion.2 = f32[384,2,704]{0,2,1:T(8,128)S(1)} fusion(bf16[384,2048,1]{1,0,2:T(8,128)(2,1)S(1)} %bitcast.70, bf16[1,2048,2,704]{1,3,2,0:T(8,128)(2,1)} %param.15), kind=kOutput, calls=%fused_computation.6 | convolution fusion | flops 2214592512 | bytes 9502720 | tf_op jit(solution)/shard_map/rd,dgf->rgf/dot_general | solution.py:30
  111.6 0.0 copy-done
  111.6 0.0 copy-start.1
  111.6 0.0 copy-start.2
  111.6 1.5 fusion.8
  113.1 0.3 copy-done.1
  113.4 0.9 fusion.14
  114.3 0.0 copy-done.2
  114.3 0.5 fusion.29
  114.8 1.3 add_convert_fusion
  116.2 0.5 fusion.39
  116.7 2.1 pad_maximum_fusion
  118.8 0.0 reduce-scatter.2.cloned.1.call-update
  119.5 138.7 %reduce-scatter.2.cloned.1.call-done = bf16[1,128,512]{2,1,0:T(8,128)(2,1)} async-done(((bf16[32,128,512]{2,1,0:T(8,128)(2,1)}), bf16[1,128,512]{2,1,0:T(8,128)(2,1)}) %reduce-scatter.2.cloned.1.call-update) | async-done | bytes 131088 | tf_op jit(solution)/shard_map/reduce_scatter | solution.py:163
  258.3 1.6 fusion.18
  (12 shorter events, 0.1 us)
Async XLA Ops:
  6.5 105.0 %copy-start = (bf16[1,704,2048]{2,1,0:T(8,128)(2,1)S(1)}, bf16[1,704,2048]{2,1,0:T(8,128)(2,1)}, u32[]{:S(2)}) copy-start(bf16[1,704,2048]{2,1,0:T(8,128)(2,1)} %param.16) | copy-start | bytes 8650756
  6.5 68.5 %all-gather.3.cloned.1.call-start = ((), (), s32[]{:S(2)}) async-start(), calls=%async_computation.2 | async-start | bytes 4325376 | tf_op jit(solution)/shard_map/all_gather | solution.py:126
  7.3 251.0 %reduce-scatter.2.cloned.1.call-start = ((), (), s32[]{:S(2)}) async-start(), calls=%async_computation.1 | async-start | bytes 4325376 | tf_op jit(solution)/shard_map/reduce_scatter | solution.py:163
  83.1 3.1 %copy-start.4 = (bf16[2048,8]{0,1:T(8,128)(2,1)S(1)}, bf16[2048,8]{0,1:T(8,128)(2,1)}, u32[]{:S(2)}) copy-start(bf16[2048,8]{0,1:T(8,128)(2,1)} %param.12) | copy-start | bytes 98308
  83.1 3.1 %copy-start.5 = (f32[2048]{0:T(1024)S(1)}, f32[2048]{0:T(1024)}, u32[]{:S(2)}) copy-start(f32[2048]{0:T(1024)} %param.11) | copy-start | bytes 24580
  111.6 1.8 copy-start.1
  111.6 2.7 %copy-start.2 = (bf16[352,2048]{1,0:T(8,128)(2,1)S(1)}, bf16[352,2048]{1,0:T(8,128)(2,1)}, u32[]{:S(2)}) copy-start(bf16[352,2048]{1,0:T(8,128)(2,1)} %param.14) | copy-start | bytes 4325380
  118.8 139.4 %copy-start.3 = (bf16[128,512]{1,0:T(8,128)(2,1)S(1)}, bf16[128,512]{1,0:T(8,128)(2,1)}, u32[]{:S(2)}) copy-start(bf16[128,512]{1,0:T(8,128)(2,1)} %param.10) | copy-start | bytes 393220
Sparse Core Ops, SparseCore 0:
  10.2 64.8 all-gather.2
  119.0 139.2 reduce-scatter.1

commit v2 on v0

--- a/solution.py
+++ b/solution.py
@@ -1,6 +1,9 @@
+import functools
 import jax
 import jax.numpy as jnp
 from jax import lax
+from jax.experimental import pallas as pl
+from jax.experimental.pallas import tpu as pltpu
 from jax.sharding import PartitionSpec as P
 
 
@@ -37,7 +40,7 @@
     return result.reshape(shape_in)
 
 
-def local(
+def local_exchange(
     hidden_in,
     norm_gain,
     router_weight,
@@ -101,6 +104,396 @@
     return mixed_out.astype(jnp.bfloat16)
 
 
+def dot_nt(a, b):
+    return lax.dot_general(a, b, (((1,), (1,)), ((), ())), preferred_element_type=jnp.float32)
+
+
+def dot_nn(a, b):
+    return jnp.dot(a, b, preferred_element_type=jnp.float32)
+
+
+def silu_mul(g, u):
+    return (g / (1.0 + jnp.exp(-g)) * u).astype(jnp.bfloat16)
+
+
+def chunks(total, step):
+    return [(at, min(step, total - at)) for at in range(0, total, step)]
+
+
+def block_kernel(
+    nz,
+    cap,
+    top,
+    hid,
+    ch_own,
+    slot_col,
+    gain,
+    router_t,
+    w_gu,
+    w_d,
+    w_sgu,
+    w_sd,
+    out,
+    xbuf,
+    cbuf,
+    gu,
+    dn,
+    sgu,
+    sdn,
+    hits,
+    member,
+    cho,
+    chg,
+    raw,
+    sel,
+    hmid,
+    expo,
+    own,
+    hsh,
+    shp,
+    keep,
+    snd,
+    crecv,
+    dsum,
+    ry0,
+    rx1,
+    xs,
+    ys,
+    rxf,
+    ryf,
+    osum,
+    rz,
+    wsem,
+    ssem,
+    rsem,
+):
+    bf16, f32 = jnp.bfloat16, jnp.float32
+    ep, tp = lax.axis_index("ep"), lax.axis_index("tp")
+    z, x, y, c = ep // 2, ep % 2, tp // 2, tp % 2
+    tok, width = hid.shape
+    half = tok // 2
+    feat = gain.shape[1]
+    slots = slot_col.shape[0]
+    me = ep * 4 + tp
+
+    def at_ep(j, i):
+        return lax.rem(z + j, nz) * 2 + (1 - x if i else x)
+
+    def at_tp(k, l):
+        return (1 - y if k else y) * 2 + (1 - c if l else c)
+
+    def cols(k, l):
+        return pl.ds(pl.multiple_of(at_tp(k, l) * width, width), width)
+
+    x_dev, y_dev, c_dev = (at_ep(0, 1), tp), (ep, at_tp(1, 0)), (ep, at_tp(0, 1))
+    peers = [(j, i) for j in range(nz) for i in range(2) if j or i]
+
+    barrier = pltpu.get_barrier_semaphore()
+    for j, i in peers:
+        pl.semaphore_signal(
+            barrier, inc=1, device_id=(at_ep(j, i), tp), device_id_type=pl.DeviceIdType.MESH
+        )
+    for dev in (y_dev, c_dev):
+        pl.semaphore_signal(barrier, inc=1, device_id=dev, device_id_type=pl.DeviceIdType.MESH)
+    loads = [
+        pltpu.make_async_copy(src, dst, wsem.at[n])
+        for n, (src, dst) in enumerate(((w_sgu, sgu), (w_sd, sdn), (w_gu, gu), (w_d, dn)))
+    ]
+    for load in loads:
+        load.start()
+    pl.semaphore_wait(barrier, len(peers) + 2)
+
+    copies = {}
+
+    def send(name, src, dst, dev):
+        n = len(copies)
+        copy = pltpu.make_async_remote_copy(
+            src_ref=src,
+            dst_ref=dst,
+            send_sem=ssem.at[n],
+            recv_sem=rsem.at[n],
+            device_id=dev,
+            device_id_type=pl.DeviceIdType.MESH,
+        )
+        copy.start()
+        copies[name] = copy
+
+    def got(*name):
+        copies[name].wait_recv()
+
+    back = lambda j: (nz - j) % nz
+    lo, hi = pl.ds(0, half), pl.ds(half, half)
+
+    for j in range(1, nz):
+        send(("z", back(j)), hid, xbuf.at[back(j), 0, 0, 0], (at_ep(j, 0), tp))
+    for j, i in peers:
+        send(("ch", back(j), i), ch_own, cbuf.at[back(j) * 2 + i], (at_ep(j, i), tp))
+
+    def spread(j):
+        if j:
+            got("z", j)
+        src = xbuf.at[j, 0, 0, 0] if j else hid
+        send(("x1", j), src, xbuf.at[j, 1, 0, 0], x_dev)
+        send(("y1", j), src, xbuf.at[j, 0, 1, 0], y_dev)
+        send(("c00", j), src, xbuf.at[j, 0, 0, 1], c_dev)
+
+    def forward(j):
+        got("x1", j)
+        send(("y2", j), xbuf.at[j, 1, 0, 0, lo], xbuf.at[j, 1, 1, 0, lo], y_dev)
+        send(("c10", j), xbuf.at[j, 1, 0, 0], xbuf.at[j, 1, 0, 1], c_dev)
+        got("y1", j)
+        send(("x2", j), xbuf.at[j, 0, 1, 0, hi], xbuf.at[j, 1, 1, 0, hi], x_dev)
+        send(("c01", j), xbuf.at[j, 0, 1, 0], xbuf.at[j, 0, 1, 1], c_dev)
+
+    def finish(j):
+        got("y2", j)
+        got("x2", j)
+        send(("c11", j), xbuf.at[j, 1, 1, 0], xbuf.at[j, 1, 1, 1], c_dev)
+
+    def select():
+        cbuf[0] = ch_own[...]
+        for j, i in peers:
+            got("ch", j, i)
+        slot_ids = lax.broadcasted_iota(jnp.int32, (slots, tok), 0)
+        place = lax.broadcasted_iota(jnp.int32, (cap, tok), 0).astype(f32)
+        members = []
+        for q in range(2 * nz):
+            picks = cbuf[q]
+            named = jnp.zeros((slots, tok), f32)
+            for k in range(top):
+                named = jnp.where(picks[k : k + 1, :] == slot_ids, 1.0, named)
+            hits[q : q + 1, :] = jnp.sum(
+                jnp.where(slot_ids == me, named, 0.0), axis=0, keepdims=True
+            )
+            members.append(named.astype(bf16))
+        earlier = lax.broadcasted_iota(jnp.int32, (tok, tok), 0) < lax.broadcasted_iota(
+            jnp.int32, (tok, tok), 1
+        )
+        hit = hits[...]
+        pos = dot_nn(hit.astype(bf16), jnp.where(earlier, 1.0, 0.0).astype(bf16))
+        for q in range(2 * nz):
+            chosen = jnp.where(place == pos[q : q + 1, :], hit[q : q + 1, :], 0.0).astype(bf16)
+            cho[q] = chosen
+            member[q * cap : (q + 1) * cap, :] = dot_nt(chosen, members[q])
+
+    def norm(v):
+        scale = lax.rsqrt(jnp.sum(v * v, axis=1, keepdims=True) * (1.0 / feat) + 1e-06)
+        return (v * scale * gain[...]).astype(bf16)
+
+    def pick(j, i):
+        q = j * 2 + i
+        for k in range(2):
+            for l in range(2):
+                raw[:, cols(k, l)] = dot_nn(cho[q], xbuf[j, i, k, l])
+        sel[q * cap : (q + 1) * cap, :] = norm(raw[...])
+
+    def shared():
+        for k in range(2):
+            for l in range(2):
+                shp[:, cols(k, l)] = xbuf[0, 0, k, l].astype(f32)
+        own[...] = norm(shp[...])
+        loads[0].wait()
+        ff = hsh.shape[1]
+        hsh[...] = silu_mul(dot_nt(own[...], sgu[0:ff, :]), dot_nt(own[...], sgu[ff : 2 * ff, :]))
+        loads[1].wait()
+        for at, size in chunks(feat, 512):
+            shp[:, at : at + size] = dot_nn(hsh[...], sdn[:, at : at + size])
+
+    def experts():
+        lanes = lax.broadcasted_iota(jnp.int32, (slots, router_t.shape[0]), 1)
+        table = jnp.where(slot_col[...] == lanes, 1.0, 0.0).astype(bf16)
+        by_slot = dot_nn(table, router_t[...]).astype(bf16)
+        logits = dot_nt(sel[...], by_slot)
+        named = member[...] > 0.5
+        top_logit = jnp.max(jnp.where(named, logits, -1e30), axis=1, keepdims=True)
+        weights = jnp.where(named, jnp.exp(jnp.where(named, logits - top_logit, 0.0)), 0.0)
+        total = jnp.maximum(jnp.sum(weights, axis=1, keepdims=True), 1.0)
+        slot_lane = lax.broadcasted_iota(jnp.int32, weights.shape, 1)
+        mine = jnp.sum(jnp.where(slot_lane == me, weights, 0.0), axis=1, keepdims=True)
+        gates = (mine / total).astype(bf16).astype(f32)
+        for q in range(2 * nz):
+            chg[q] = (cho[q].astype(f32) * gates[q * cap : (q + 1) * cap, :]).astype(bf16)
+        loads[2].wait()
+        ff = hmid.shape[1]
+        for at, size in chunks(ff, 256):
+            hmid[:, at : at + size] = silu_mul(
+                dot_nt(sel[...], gu[at : at + size, :]),
+                dot_nt(sel[...], gu[ff + at : ff + at + size, :]),
+            )
+        loads[3].wait()
+        for at, size in chunks(feat, 512):
+            expo[:, at : at + size] = dot_nn(hmid[...], dn[:, at : at + size]).astype(bf16)
+
+    cbuf_ready = select
+    xbuf[0, 0, 0, 0] = hid[...]
+    spread(0)
+    forward(0)
+    for j in range(1, nz):
+        spread(j)
+        if j == 1:
+            cbuf_ready()
+        forward(j)
+        finish(j - 1)
+        for name in ("c00", "c10", "c01", "c11"):
+            got(name, j - 1)
+        if j == 1:
+            shared()
+        pick(j - 1, 0)
+        pick(j - 1, 1)
+    finish(nz - 1)
+    for name in ("c00", "c10", "c01", "c11"):
+        got(name, nz - 1)
+    pick(nz - 1, 0)
+    pick(nz - 1, 1)
+    experts()
+
+    def add(*refs):
+        total = refs[0][...].astype(f32)
+        for ref in refs[1:]:
+            total = total + ref[...].astype(f32)
+        return total
+
+    def scatter(j):
+        for i in (1, 0):
+            q = j * 2 + i
+            for l in (1, 0):
+                for k in (1, 0):
+                    part = lax.dot_general(
+                        chg[q],
+                        expo[q * cap : (q + 1) * cap, cols(k, l)],
+                        (((0,), (0,)), ((), ())),
+                        preferred_element_type=f32,
+                    )
+                    if q == 0:
+                        part = part + shp[:, cols(k, l)]
+                    (snd if l else keep)[j, i, k] = part.astype(bf16)
+                if l:
+                    send(("rc", j, i), snd.at[j, i], crecv.at[j, i], c_dev)
+
+    def diagonal(j):
+        got("rc", j, 1)
+        dsum[j] = add(keep.at[j, 1, 1], crecv.at[j, 1, 1]).astype(bf16)
+        send(("d0", j), dsum.at[j, lo], ry0.at[j], y_dev)
+        send(("d1", j), dsum.at[j, hi], rx1.at[j], x_dev)
+
+    def sides(j):
+        xs[j, hi] = add(keep.at[j, 1, 0, hi], crecv.at[j, 1, 0, hi]).astype(bf16)
+        got("d0", j)
+        xs[j, lo] = add(keep.at[j, 1, 0, lo], crecv.at[j, 1, 0, lo], ry0.at[j]).astype(bf16)
+        send(("rx", j), xs.at[j], rxf.at[j], x_dev)
+        got("rc", j, 0)
+        ys[j, lo] = add(keep.at[j, 0, 1, lo], crecv.at[j, 0, 1, lo]).astype(bf16)
+        got("d1", j)
+        ys[j, hi] = add(keep.at[j, 0, 1, hi], crecv.at[j, 0, 1, hi], rx1.at[j]).astype(bf16)
+        send(("ry", j), ys.at[j], ryf.at[j], y_dev)
+
+    def gather_sum(j):
+        got("rx", j)
+        got("ry", j)
+        total = add(keep.at[j, 0, 0], crecv.at[j, 0, 0], rxf.at[j], ryf.at[j])
+        if j:
+            osum[j] = total.astype(bf16)
+            send(("rz", j), osum.at[j], rz.at[j], (at_ep(j, 0), tp))
+        else:
+            out[...] = total
+
+    order = sorted(range(1, nz), key=lambda j: -min(j, nz - j)) + [0]
+    for t in range(nz + 3):
+        for lag, stage in ((0, scatter), (1, diagonal), (2, sides), (3, gather_sum)):
+            if 0 <= t - lag < nz:
+                stage(order[t - lag])
+    for j in range(1, nz):
+        got("rz", j)
+        out[...] += rz[j].astype(f32)
+    for copy in copies.values():
+        copy.wait_send()
+
+
+def local_dense(
+    hidden_in,
+    norm_gain,
+    router_weight,
+    shared_gate_up,
+    shared_down,
+    slot_gate_up,
+    slot_down,
+    slot_expert,
+    slot_choice,
+    live_count,
+):
+    nz = lax.axis_size("ep") // 2
+    tok_count, width = hidden_in.shape
+    feat = 4 * width
+    top_count = slot_choice.shape[1]
+    slot_count = slot_expert.shape[0]
+    cap = 4 * max(2, 2 * (tok_count // 4) * top_count // slot_count)
+    rows = 2 * nz * cap
+    sff, eff = shared_down.shape[0], slot_down.shape[1]
+    choice_t = jnp.pad(slot_choice.T, ((0, 8 - top_count), (0, 0)), constant_values=-1)
+    bf16, f32 = jnp.bfloat16, jnp.float32
+    half = tok_count // 2
+    block = (tok_count, width)
+    vmem = pl.BlockSpec(memory_space=pltpu.VMEM)
+    hbm = pl.BlockSpec(memory_space=pl.ANY)
+    copy_count = (nz - 1) + (2 * nz - 1) + 3 * nz + 4 * nz + nz + 2 * nz + 4 * nz + (nz - 1)
+    summed = pl.pallas_call(
+        functools.partial(block_kernel, nz, cap, top_count),
+        out_shape=jax.ShapeDtypeStruct(block, f32),
+        in_specs=[vmem] * 5 + [hbm] * 4,
+        out_specs=vmem,
+        scratch_shapes=[
+            pltpu.VMEM((nz, 2, 2, 2) + block, bf16),
+            pltpu.VMEM((2 * nz, 8, tok_count), jnp.int32),
+            pltpu.VMEM((2 * eff, feat), bf16),
+            pltpu.VMEM((eff, feat), bf16),
+            pltpu.VMEM((2 * sff, feat), bf16),
+            pltpu.VMEM((sff, feat), bf16),
+            pltpu.VMEM((2 * nz, tok_count), f32),
+            pltpu.VMEM((rows, slot_count), f32),
+            pltpu.VMEM((2 * nz, cap, tok_count), bf16),
+            pltpu.VMEM((2 * nz, cap, tok_count), bf16),
+            pltpu.VMEM((cap, feat), f32),
+            pltpu.VMEM((rows, feat), bf16),
+            pltpu.VMEM((rows, eff), bf16),
+            pltpu.VMEM((rows, feat), bf16),
+            pltpu.VMEM((tok_count, feat), bf16),
+            pltpu.VMEM((tok_count, sff), bf16),
+            pltpu.VMEM((tok_count, feat), f32),
+            pltpu.VMEM((nz, 2, 2) + block, bf16),
+            pltpu.VMEM((nz, 2, 2) + block, bf16),
+            pltpu.VMEM((nz, 2, 2) + block, bf16),
+            pltpu.VMEM((nz,) + block, bf16),
+            pltpu.VMEM((nz, half, width), bf16),
+            pltpu.VMEM((nz, half, width), bf16),
+            pltpu.VMEM((nz,) + block, bf16),
+            pltpu.VMEM((nz,) + block, bf16),
+            pltpu.VMEM((nz,) + block, bf16),
+            pltpu.VMEM((nz,) + block, bf16),
+            pltpu.VMEM((nz,) + block, bf16),
+            pltpu.VMEM((nz,) + block, bf16),
+            pltpu.SemaphoreType.DMA((4,)),
+            pltpu.SemaphoreType.DMA((copy_count,)),
+            pltpu.SemaphoreType.DMA((copy_count,)),
+        ],
+        compiler_params=pltpu.CompilerParams(
+            collective_id=0, has_side_effects=True, vmem_limit_bytes=56 * 2**20
+        ),
+    )(
+        hidden_in,
+        choice_t,
+        slot_expert.reshape(-1, 1),
+        norm_gain.reshape(1, -1),
+        router_weight.T,
+        slot_gate_up[0].transpose(1, 2, 0).reshape(2 * eff, feat),
+        slot_down[0],
+        shared_gate_up.transpose(1, 2, 0).reshape(2 * sff, feat),
+        shared_down,
+    )
+    live_rows = jnp.arange(tok_count, dtype=jnp.int32) < live_count[0]
+    mixed_out = jnp.where(live_rows[:, None], hidden_in.astype(jnp.float32) + summed, 0.0)
+    return mixed_out.astype(jnp.bfloat16)
+
+
 def solution(mesh):
     in_specs = (
         P("ep", "tp"),
@@ -115,4 +508,5 @@
         P("ep"),
     )
     out_specs = P("ep", "tp")
+    local = local_dense if mesh.size <= 64 and mesh.shape["tp"] == 4 else local_exchange
     return jax.shard_map(local, mesh=mesh, in_specs=in_specs, out_specs=out_specs, check_vma=False)

time: 239 us -> 78.9 us (0.33)
  blocking collectives: 74.6 us -> 0 us
  waiting for transfers between devices: 74.3 us -> 0 us
  Pallas kernels: 0 us -> 73.7 us
  local copies, waits for them, and re-layouts: 46.3 us -> 2.63 us
  matrix products: 14.5 us -> 0 us
  between operations: 14.2 us -> 0.68 us
  starting transfers between devices: 9.12 us -> 0 us
  other arithmetic: 5.13 us -> 1.7 us
    pallas_call x0 -> x1, Pallas kernels: none -> 73.7 us  [local_dense(): pl.pallas_call(functools.partial(block_kernel, nz, cap, top_count), out_s...]
    all_to_all x2 -> x0, blocking collectives: 65.6 us -> none  [the longest x1 43.1 us: local(): lax.all_to_all(outgoing, 'ep', split_axis=0, concat_axis=0, tiled=True)]
    all_to_all x2 -> x0, waiting for transfers between devices: 51.8 us -> none  [the longest x1 36.6 us: local(): lax.all_to_all(computed, 'ep', split_axis=0, concat_axis=0, tiled=True)]
    reshape x8 -> x1, local copies, waits for them, and re-layouts: 25.6 us -> 1.34 us  [local_dense(): slot_expert.reshape(-1, 1)]
    reduce_scatter x1 -> x0, waiting for transfers between devices: 22.5 us -> none  [local(): lax.psum_scatter(partial_value, 'tp', scatter_dimension=1, tiled=True)]
    dot_general x6 -> x0, matrix products: 14.5 us -> none  [the longest x1 5.65 us: expert_apply(): jnp.einsum('rd,dgf->rgf', flat_rows, slot_gate_up[0], preferred_element_t...]
    all_to_all x4 -> x0, local copies, waits for them, and re-layouts: 10.1 us -> none  [the longest x1 3.62 us: local(): lax.all_to_all(lax.all_to_all(computed, 'ep', split_axis=0, concat_axis=0...]
    all_to_all x2 -> x0, starting transfers between devices: 9.08 us -> none  [the longest x1 4.6 us: local(): lax.all_to_all(computed, 'ep', split_axis=0, concat_axis=0, tiled=True)]
  transfers between devices with their start and end apart: 3 -> 0, of which waited for: 3 -> 0; matrix products, arithmetic and copies ran while one was open for 2% -> 0% of each run, Pallas kernels for 0% -> 0%
where the time goes in v2:
time: 78.9 us; the launch traced here: 78.7 us
  Pallas kernels  73.7 us (93%)
  local copies, waits for them, and re-layouts  2.63 us (3%)
  other arithmetic  1.7 us (2%)
    pallas_call x1, Pallas kernels, local_dense(): pl.pallas_call(functools.partial(block_kernel, nz, cap, top_count), out_s...  73.7 us
    convert_element_type x1, other arithmetic, local_dense(): return mixed_out.astype(jnp.bfloat16)  1.69 us

profile of v2, /device:TPU:0, one launch (start us, length us, event | category | flops | bytes accessed | tf_op | source)
XLA Modules:
  0.0 78.7 jit_solution(4764681047840605313)
XLA Ops:
  0.7 1.3 %pad.4.ch_own = s32[8,128]{1,0:T(8,128)} pad(s32[6,128]{1,0:T(8,128)} %bitcast.20, s32[]{:T(128)} %constant.0.clone.1), padding=0_2x0_0 | pad | bytes 7172 | tf_op jit(solution)/shard_map/jit(_pad)/pad | solution.py:432
  2.0 1.3 %copy.11.slot_col = s32[32,1]{1,0:T(8,128)} copy(s32[32,1]{0,1:T(1,128)} %bitcast.21) | data formatting | bytes 256 | tf_op jit(solution)/shard_map/reshape | solution.py:484
  3.3 0.0 copy-start
  3.3 73.7 %shard_map.100 = f32[128,512]{1,0:T(8,128)} custom-call(bf16[128,512]{1,0:T(8,128)(2,1)} %hid.1, s32[8,128]{1,0:T(8,128)} %pad.4.ch_own, s32[32,1]{1,0:T(8,128)} %copy.11.slot_col, f32[1,2048]{1,0:T(1,128)} %bitcast.19, bf16[8,2048]{1,0:T(8,128)(2,1)} %bitcast.18, bf16[1408,2048]{1,0:T(8,128)(2,1)} %bitcast.15, bf16[704,2048]{1,0:T(8,128)(2,1)} %bitcast.16, ...), custom_call_target="tpu_custom_call" | custom-call | tf_op jit(solution)/shard_map/pallas_call | solution.py:439
  77.0 0.0 copy-done
  77.0 1.7 %select_convert_fusion = bf16[128,512]{1,0:T(8,128)(2,1)} fusion(f32[128,512]{1,0:T(8,128)} %shard_map.100, bf16[128,512]{1,0:T(8,128)(2,1)S(1)} %copy-done, pred[128]{0:T(512)(128)(4,1)S(1)} %iota_compare_fusion), kind=kLoop, calls=%fused_computation | loop fusion | flops 262144 | bytes 524416 | tf_op jit(solution)/shard_map/convert_element_type | solution.py:494
  (1 shorter events, 0.0 us)
Async XLA Ops:
  3.3 73.7 %copy-start = (bf16[128,512]{1,0:T(8,128)(2,1)S(1)}, bf16[128,512]{1,0:T(8,128)(2,1)}, u32[]{:S(2)}) copy-start(bf16[128,512]{1,0:T(8,128)(2,1)} %hid.1) | copy-start | bytes 393220

commit v3 on v2

--- a/solution.py
+++ b/solution.py
@@ -126,7 +126,7 @@
     top,
     hid,
     ch_own,
-    slot_col,
+    slot_row,
     gain,
     router_t,
     w_gu,
@@ -141,6 +141,7 @@
     sgu,
     sdn,
     hits,
+    by_slot,
     member,
     cho,
     chg,
@@ -173,7 +174,7 @@
     tok, width = hid.shape
     half = tok // 2
     feat = gain.shape[1]
-    slots = slot_col.shape[0]
+    slots = slot_row.shape[1]
     me = ep * 4 + tp
 
     def at_ep(j, i):
@@ -199,8 +200,6 @@
         pltpu.make_async_copy(src, dst, wsem.at[n])
         for n, (src, dst) in enumerate(((w_sgu, sgu), (w_sd, sdn), (w_gu, gu), (w_d, dn)))
     ]
-    for load in loads:
-        load.start()
     pl.semaphore_wait(barrier, len(peers) + 2)
 
     copies = {}
@@ -224,10 +223,16 @@
     back = lambda j: (nz - j) % nz
     lo, hi = pl.ds(0, half), pl.ds(half, half)
 
-    for j in range(1, nz):
-        send(("z", back(j)), hid, xbuf.at[back(j), 0, 0, 0], (at_ep(j, 0), tp))
-    for j, i in peers:
-        send(("ch", back(j), i), ch_own, cbuf.at[back(j) * 2 + i], (at_ep(j, i), tp))
+    order = sorted(range(nz), key=lambda j: min(j, nz - j))
+    pos = {j: n for n, j in enumerate(order)}
+
+    def send_rows():
+        for j in order[1:]:
+            send(("z", j), hid, xbuf.at[j, 0, 0, 0], (at_ep(back(j), 0), tp))
+
+    def send_choices():
+        for j, i in peers:
+            send(("ch", j, i), ch_own, cbuf.at[pos[j] * 2 + i], (at_ep(back(j), i), tp))
 
     def spread(j):
         if j:
@@ -270,18 +275,23 @@
             jnp.int32, (tok, tok), 1
         )
         hit = hits[...]
-        pos = dot_nn(hit.astype(bf16), jnp.where(earlier, 1.0, 0.0).astype(bf16))
+        rank = dot_nn(hit.astype(bf16), jnp.where(earlier, 1.0, 0.0).astype(bf16))
         for q in range(2 * nz):
-            chosen = jnp.where(place == pos[q : q + 1, :], hit[q : q + 1, :], 0.0).astype(bf16)
+            chosen = jnp.where(place == rank[q : q + 1, :], hit[q : q + 1, :], 0.0).astype(bf16)
             cho[q] = chosen
             member[q * cap : (q + 1) * cap, :] = dot_nt(chosen, members[q])
+        held = lax.broadcasted_iota(jnp.int32, (router_t.shape[0], slots), 0)
+        table = jnp.where(slot_row[...] == held, 1.0, 0.0).astype(bf16)
+        by_slot[...] = lax.dot_general(
+            table, router_t[...], (((0,), (0,)), ((), ())), preferred_element_type=f32
+        ).astype(bf16)
 
     def norm(v):
         scale = lax.rsqrt(jnp.sum(v * v, axis=1, keepdims=True) * (1.0 / feat) + 1e-06)
         return (v * scale * gain[...]).astype(bf16)
 
     def pick(j, i):
-        q = j * 2 + i
+        q = pos[j] * 2 + i
         for k in range(2):
             for l in range(2):
                 raw[:, cols(k, l)] = dot_nn(cho[q], xbuf[j, i, k, l])
@@ -299,53 +309,40 @@
         for at, size in chunks(feat, 512):
             shp[:, at : at + size] = dot_nn(hsh[...], sdn[:, at : at + size])
 
-    def experts():
-        lanes = lax.broadcasted_iota(jnp.int32, (slots, router_t.shape[0]), 1)
-        table = jnp.where(slot_col[...] == lanes, 1.0, 0.0).astype(bf16)
-        by_slot = dot_nn(table, router_t[...]).astype(bf16)
-        logits = dot_nt(sel[...], by_slot)
-        named = member[...] > 0.5
+    def experts(js):
+        first, last = 2 * min(pos[j] for j in js), 2 * max(pos[j] for j in js) + 2
+        part = slice(first * cap, last * cap)
+        logits = dot_nt(sel[part, :], by_slot[...])
+        named = member[part, :] > 0.5
         top_logit = jnp.max(jnp.where(named, logits, -1e30), axis=1, keepdims=True)
         weights = jnp.where(named, jnp.exp(jnp.where(named, logits - top_logit, 0.0)), 0.0)
         total = jnp.maximum(jnp.sum(weights, axis=1, keepdims=True), 1.0)
         slot_lane = lax.broadcasted_iota(jnp.int32, weights.shape, 1)
         mine = jnp.sum(jnp.where(slot_lane == me, weights, 0.0), axis=1, keepdims=True)
         gates = (mine / total).astype(bf16).astype(f32)
-        for q in range(2 * nz):
-            chg[q] = (cho[q].astype(f32) * gates[q * cap : (q + 1) * cap, :]).astype(bf16)
-        loads[2].wait()
+        for q in range(first, last):
+            at = (q - first) * cap
+            chg[q] = (cho[q].astype(f32) * gates[at : at + cap, :]).astype(bf16)
+        if first == 0:
+            loads[2].wait()
         ff = hmid.shape[1]
         for at, size in chunks(ff, 256):
-            hmid[:, at : at + size] = silu_mul(
-                dot_nt(sel[...], gu[at : at + size, :]),
-                dot_nt(sel[...], gu[ff + at : ff + at + size, :]),
+            hmid[part, at : at + size] = silu_mul(
+                dot_nt(sel[part, :], gu[at : at + size, :]),
+                dot_nt(sel[part, :], gu[ff + at : ff + at + size, :]),
             )
-        loads[3].wait()
+        if first == 0:
+            loads[3].wait()
         for at, size in chunks(feat, 512):
-            expo[:, at : at + size] = dot_nn(hmid[...], dn[:, at : at + size]).astype(bf16)
-
-    cbuf_ready = select
-    xbuf[0, 0, 0, 0] = hid[...]
-    spread(0)
-    forward(0)
-    for j in range(1, nz):
-        spread(j)
-        if j == 1:
-            cbuf_ready()
-        forward(j)
-        finish(j - 1)
+            expo[part, at : at + size] = dot_nn(hmid[part, :], dn[:, at : at + size]).astype(bf16)
+
+    def take(j):
         for name in ("c00", "c10", "c01", "c11"):
-            got(name, j - 1)
-        if j == 1:
+            got(name, j)
+        if j == 0:
             shared()
-        pick(j - 1, 0)
-        pick(j - 1, 1)
-    finish(nz - 1)
-    for name in ("c00", "c10", "c01", "c11"):
-        got(name, nz - 1)
-    pick(nz - 1, 0)
-    pick(nz - 1, 1)
-    experts()
+        pick(j, 0)
+        pick(j, 1)
 
     def add(*refs):
         total = refs[0][...].astype(f32)
@@ -355,7 +352,7 @@
 
     def scatter(j):
         for i in (1, 0):
-            q = j * 2 + i
+            q = pos[j] * 2 + i
             for l in (1, 0):
                 for k in (1, 0):
                     part = lax.dot_general(
@@ -397,11 +394,33 @@
         else:
             out[...] = total
 
-    order = sorted(range(1, nz), key=lambda j: -min(j, nz - j)) + [0]
+    xbuf[0, 0, 0, 0] = hid[...]
+    spread(0)
+    send_rows()
+    send_choices()
+    for load in loads:
+        load.start()
+    group = []
+    back_order = order[1:] + order[:1]
+    done = 0
+    for t in range(nz + 3):
+        for lag, stage in ((0, spread), (1, forward), (2, finish), (3, take)):
+            if (lag == 0 and 0 < t < nz) or (lag and 0 <= t - lag < nz):
+                stage(order[t - lag])
+        if t == 1:
+            select()
+        if t >= 3:
+            group.append(order[t - 3])
+            if len(group) == 2:
+                experts(group)
+                group = []
+        if t == nz + 1 and 1:
+            scatter(back_order[0])
+            done = 1
     for t in range(nz + 3):
         for lag, stage in ((0, scatter), (1, diagonal), (2, sides), (3, gather_sum)):
-            if 0 <= t - lag < nz:
-                stage(order[t - lag])
+            if 0 <= t - lag < nz and (lag or t >= done):
+                stage(back_order[t - lag])
     for j in range(1, nz):
         got("rz", j)
         out[...] += rz[j].astype(f32)
@@ -429,7 +448,6 @@
     cap = 4 * max(2, 2 * (tok_count // 4) * top_count // slot_count)
     rows = 2 * nz * cap
     sff, eff = shared_down.shape[0], slot_down.shape[1]
-    choice_t = jnp.pad(slot_choice.T, ((0, 8 - top_count), (0, 0)), constant_values=-1)
     bf16, f32 = jnp.bfloat16, jnp.float32
     half = tok_count // 2
     block = (tok_count, width)
@@ -443,12 +461,13 @@
         out_specs=vmem,
         scratch_shapes=[
             pltpu.VMEM((nz, 2, 2, 2) + block, bf16),
-            pltpu.VMEM((2 * nz, 8, tok_count), jnp.int32),
+            pltpu.VMEM((2 * nz, top_count, tok_count), jnp.int32),
             pltpu.VMEM((2 * eff, feat), bf16),
             pltpu.VMEM((eff, feat), bf16),
             pltpu.VMEM((2 * sff, feat), bf16),
             pltpu.VMEM((sff, feat), bf16),
             pltpu.VMEM((2 * nz, tok_count), f32),
+            pltpu.VMEM((slot_count, feat), bf16),
             pltpu.VMEM((rows, slot_count), f32),
             pltpu.VMEM((2 * nz, cap, tok_count), bf16),
             pltpu.VMEM((2 * nz, cap, tok_count), bf16),
@@ -480,8 +499,8 @@
         ),
     )(
         hidden_in,
-        choice_t,
-        slot_expert.reshape(-1, 1),
+        slot_choice.T,
+        slot_expert.reshape(1, -1),
         norm_gain.reshape(1, -1),
         router_weight.T,
         slot_gate_up[0].transpose(1, 2, 0).reshape(2 * eff, feat),

time: 78.9 us -> 68 us (0.86)
  Pallas kernels: 73.7 us -> 65.4 us
  local copies, waits for them, and re-layouts: 2.63 us -> 0.01 us
    pallas_call x1, Pallas kernels: 73.7 us -> 65.4 us  [local_dense(): pl.pallas_call(functools.partial(block_kernel, nz, cap, top_count), out_s...]
    reshape x1 -> x0, local copies, waits for them, and re-layouts: 1.34 us -> none  [local_dense(): slot_expert.reshape(-1, 1)]
    pad x1 -> x0, local copies, waits for them, and re-layouts: 1.29 us -> none  [local_dense(): jnp.pad(slot_choice.T, ((0, 8 - top_count), (0, 0)), constant_values=-1)]
where the time goes in v3:
time: 68 us; the launch traced here: 67.8 us
  Pallas kernels  65.4 us (96%)
  other arithmetic  1.7 us (2%)
  between operations  0.68 us (1%)
    pallas_call x1, Pallas kernels, local_dense(): pl.pallas_call(functools.partial(block_kernel, nz, cap, top_count), out_s...  65.4 us
    convert_element_type x1, other arithmetic, local_dense(): return mixed_out.astype(jnp.bfloat16)  1.69 us

profile of v3, /device:TPU:0, one launch (start us, length us, event | category | flops | bytes accessed | tf_op | source)
XLA Modules:
  0.0 67.8 jit_solution(1313207543894840929)
XLA Ops:
  0.7 0.0 copy-start
  0.7 65.4 %shard_map.100 = f32[128,512]{1,0:T(8,128)} custom-call(bf16[128,512]{1,0:T(8,128)(2,1)} %hid.1, s32[6,128]{1,0:T(8,128)} %bitcast.20, s32[1,32]{1,0:T(1,128)} %bitcast.21, f32[1,2048]{1,0:T(1,128)} %bitcast.19, bf16[8,2048]{1,0:T(8,128)(2,1)} %bitcast.18, bf16[1408,2048]{1,0:T(8,128)(2,1)} %bitcast.15, bf16[704,2048]{1,0:T(8,128)(2,1)} %bitcast.16, ...), custom_call_target="tpu_custom_call" | custom-call | tf_op jit(solution)/shard_map/pallas_call | solution.py:457
  66.1 0.0 copy-done
  66.1 1.7 %select_convert_fusion = bf16[128,512]{1,0:T(8,128)(2,1)} fusion(f32[128,512]{1,0:T(8,128)} %shard_map.100, bf16[128,512]{1,0:T(8,128)(2,1)S(1)} %copy-done, pred[128]{0:T(512)(128)(4,1)S(1)} %iota_compare_fusion), kind=kLoop, calls=%fused_computation | loop fusion | flops 262144 | bytes 524416 | tf_op jit(solution)/shard_map/convert_element_type | solution.py:513
  (1 shorter events, 0.0 us)
Async XLA Ops:
  0.7 65.5 %copy-start = (bf16[128,512]{1,0:T(8,128)(2,1)S(1)}, bf16[128,512]{1,0:T(8,128)(2,1)}, u32[]{:S(2)}) copy-start(bf16[128,512]{1,0:T(8,128)(2,1)} %hid.1) | copy-start | bytes 393220

commit v4 on v3

--- a/solution.py
+++ b/solution.py
@@ -164,6 +164,7 @@
     ryf,
     osum,
     rz,
+    own_sum,
     wsem,
     ssem,
     rsem,
@@ -351,9 +352,9 @@
         return total
 
     def scatter(j):
-        for i in (1, 0):
-            q = pos[j] * 2 + i
-            for l in (1, 0):
+        for l in (1, 0):
+            for i in (1, 0):
+                q = pos[j] * 2 + i
                 for k in (1, 0):
                     part = lax.dot_general(
                         chg[q],
@@ -392,7 +393,7 @@
             osum[j] = total.astype(bf16)
             send(("rz", j), osum.at[j], rz.at[j], (at_ep(j, 0), tp))
         else:
-            out[...] = total
+            own_sum[...] = total
 
     xbuf[0, 0, 0, 0] = hid[...]
     spread(0)
@@ -407,7 +408,7 @@
         for lag, stage in ((0, spread), (1, forward), (2, finish), (3, take)):
             if (lag == 0 and 0 < t < nz) or (lag and 0 <= t - lag < nz):
                 stage(order[t - lag])
-        if t == 1:
+        if t == 2:
             select()
         if t >= 3:
             group.append(order[t - 3])
@@ -423,7 +424,10 @@
                 stage(back_order[t - lag])
     for j in range(1, nz):
         got("rz", j)
-        out[...] += rz[j].astype(f32)
+    total = hid[...].astype(f32) + own_sum[...]
+    for j in range(1, nz):
+        total = total + rz[j].astype(f32)
+    out[...] = total.astype(bf16)
     for copy in copies.values():
         copy.wait_send()
 
@@ -454,9 +458,9 @@
     vmem = pl.BlockSpec(memory_space=pltpu.VMEM)
     hbm = pl.BlockSpec(memory_space=pl.ANY)
     copy_count = (nz - 1) + (2 * nz - 1) + 3 * nz + 4 * nz + nz + 2 * nz + 4 * nz + (nz - 1)
-    summed = pl.pallas_call(
+    mixed = pl.pallas_call(
         functools.partial(block_kernel, nz, cap, top_count),
-        out_shape=jax.ShapeDtypeStruct(block, f32),
+        out_shape=jax.ShapeDtypeStruct(block, bf16),
         in_specs=[vmem] * 5 + [hbm] * 4,
         out_specs=vmem,
         scratch_shapes=[
@@ -490,6 +494,7 @@
             pltpu.VMEM((nz,) + block, bf16),
             pltpu.VMEM((nz,) + block, bf16),
             pltpu.VMEM((nz,) + block, bf16),
+            pltpu.VMEM(block, f32),
             pltpu.SemaphoreType.DMA((4,)),
             pltpu.SemaphoreType.DMA((copy_count,)),
             pltpu.SemaphoreType.DMA((copy_count,)),
@@ -509,8 +514,7 @@
         shared_down,
     )
     live_rows = jnp.arange(tok_count, dtype=jnp.int32) < live_count[0]
-    mixed_out = jnp.where(live_rows[:, None], hidden_in.astype(jnp.float32) + summed, 0.0)
-    return mixed_out.astype(jnp.bfloat16)
+    return jnp.where(live_rows[:, None], mixed, jnp.zeros_like(mixed))
 
 
 def solution(mesh):

time: 68 us -> 63.7 us (0.937)
  Pallas kernels: 65.4 us -> 61.2 us
    pallas_call x1, Pallas kernels: 65.4 us -> 61.2 us  [local_dense(): pl.pallas_call(functools.partial(block_kernel, nz, cap, top_count), out_s...]
    convert_element_type x1 -> x0, other arithmetic: 1.69 us -> none  [local_dense(): return mixed_out.astype(jnp.bfloat16)]
    select_n x0 -> x1, other arithmetic: none -> 1.65 us  [local_dense(): return jnp.where(live_rows[:, None], mixed, jnp.zeros_like(mixed))]
where the time goes in v4:
time: 63.7 us; the launch traced here: 63.5 us
  Pallas kernels  61.2 us (96%)
  other arithmetic  1.65 us (3%)
  between operations  0.67 us (1%)
    pallas_call x1, Pallas kernels, local_dense(): pl.pallas_call(functools.partial(block_kernel, nz, cap, top_count), out_s...  61.2 us
    select_n x1, other arithmetic, local_dense(): return jnp.where(live_rows[:, None], mixed, jnp.zeros_like(mixed))  1.65 us

profile of v4, /device:TPU:0, one launch (start us, length us, event | category | flops | bytes accessed | tf_op | source)
XLA Modules:
  0.0 63.5 jit_solution(16285707108966109349)
XLA Ops:
  0.7 61.2 %shard_map.100 = bf16[128,512]{1,0:T(8,128)(2,1)} custom-call(bf16[128,512]{1,0:T(8,128)(2,1)} %hid.1, s32[6,128]{1,0:T(8,128)} %bitcast.20, s32[1,32]{1,0:T(1,128)} %bitcast.21, f32[1,2048]{1,0:T(1,128)} %bitcast.19, bf16[8,2048]{1,0:T(8,128)(2,1)} %bitcast.18, bf16[1408,2048]{1,0:T(8,128)(2,1)} %bitcast.15, bf16[704,2048]{1,0:T(8,128)(2,1)} %bitcast.16, ...), custom_call_target="tpu_custom_call" | custom-call | tf_op jit(solution)/shard_map/pallas_call | solution.py:461
  61.9 1.6 %broadcast_select_fusion = bf16[128,512]{1,0:T(8,128)(2,1)} fusion(bf16[128,512]{1,0:T(8,128)(2,1)} %shard_map.100, pred[128]{0:T(512)(128)(4,1)S(1)} %iota_compare_fusion), kind=kLoop, calls=%fused_computation | loop fusion | flops 65536 | bytes 262272 | tf_op jit(solution)/shard_map/jit(_where)/select_n | solution.py:517
  (1 shorter events, 0.0 us)
